TPU v7x, 128 devices: a whole 4x4x4 slice. The times are simulated.
128 devices in a mesh: seq: 16 (over x_lo, y, core), heads: 8 (over z, x_hi).
Axes of the slice: x: 4 (x_hi: 2, x_lo: 2; x = x_hi * 2 + x_lo), y: 4, z: 4, core: 2. Of those that a mesh axis runs over, the one named last changes fastest.
Arguments:
- hidden_in: bfloat16 [4096, 8192], P('seq', 'heads'), may hold values from -6 to 6
- queries: bfloat16 [4096, 8192], P('seq', 'heads'), as said below
- image_kv: bfloat16 [16, 2, 6528, 1024], P('seq', None, None, 'heads'), as said below
- out_weight: bfloat16 [8192, 8192], P('seq', 'heads'), may hold values from -0.0625 to 0.0625
- gate: float32 [1], replicated, may hold values from 0.4 to 1.2
- tile_counts: int32 [16], replicated, may hold values from 1 to 4, as said below
- owners: int32 [256], replicated, may hold values from 0 to 15, as said below
- starts: int32 [256], replicated, may hold values from 0 to 3, as said below
- norm_gain: float32 [8192], P('heads'), may hold values from 0.1 to 1.9
- norm_grad: bfloat16 [4096, 8192], P('seq', 'heads'), may hold values from -6 to 6
- stream_grad: bfloat16 [4096, 8192], P('seq', 'heads'), may hold values from -6 to 6
Outputs:
- hidden_out: bfloat16 [4096, 8192], P('seq', 'heads')
- stream_in_grad: float32 [4096, 8192], P('seq', 'heads')
Inputs may be any that keep to these rules, and one draw needn't show every extreme that they name: `tile_counts`: tiles of each image; some image has 4 tiles in every draw. `owners`: the image (named by the seq index that owns it) that a block of 16 text rows attends to; of the 16 blocks of one seq index at most 2 name the same image, and in every draw some image is named by exactly 2 blocks of every seq index. `starts`: the first tile a block sees, below the tile count of the block's image; in every draw some block starts at tile 0 and some at tile 4 - 1. `image_kv`: keys and values are real-valued. real-valued queries.
All inputs are finite; a program needn't handle non-finite values.
Results may differ from a plain program's by a relative error of at most 0.007.
Values may be sent and summed in bfloat16 or wider, within the bound.
No kernel may reach another device: no remote copies, remote signals or barrier semaphores. Data moves between devices by JAX's collectives and lax.ppermute only.
A program may use at most 128 MiB of HBM per device.

v0:
```python
import functools
import math

import jax
import jax.numpy as jnp
from jax import lax
from jax.experimental import pallas as pl
from jax.experimental.pallas import tpu as pltpu
from jax.sharding import Mesh, PartitionSpec as P


D = 8192
HEAD_DIM = 128
TILE_TOK = 1601
TILE_STEP = 1600
KEY_CAP = 6528
KEY_BLK = 1664
BLOCKS_DEV = 16
CAP = 2
BLK = 16
SEQ = 16
SLOTS = SEQ * CAP
HEADS_DEV = 8
GROUP = 8
SUB = 512
LOW = -2.3e38
HIGH = 2.3e38
EPS = 1e-05
EXP2_SCALE = math.log2(math.e) / math.sqrt(HEAD_DIM)

SEQ_AXES = ("xl", "y", "core")
HEAD_AXES = ("z", "xh")
UP = [(i, (i + 1) % 4) for i in range(4)]
DOWN = [(i, (i - 1) % 4) for i in range(4)]
SWAP = [(0, 1), (1, 0)]


def vmem():
    return pl.BlockSpec(memory_space=pltpu.VMEM)


def smem():
    return pl.BlockSpec(memory_space=pltpu.SMEM)


def near(*arrays):
    return [pltpu.with_memory_space_constraint(x, pltpu.VMEM) for x in arrays]


LIMIT = pltpu.CompilerParams(vmem_limit_bytes=24 << 20)
SMALL = pltpu.CompilerParams(vmem_limit_bytes=8 << 20)


def dispatch_kernel(owner_ref, q_ref, out_ref, used):
    first = lax.axis_index(SEQ_AXES) * BLOCKS_DEV
    for o in range(SEQ):
        used[o] = 0

    def place(b, carry):
        o = owner_ref[first + b]
        r = used[o]
        used[o] = r + 1
        row = pl.multiple_of(b * BLK, BLK)
        out_ref[o, r] = q_ref[pl.ds(row, BLK), :]
        return carry

    lax.fori_loop(0, BLOCKS_DEV, place, 0)


def dispatch(owners, queries):
    return pl.pallas_call(
        dispatch_kernel,
        out_shape=pltpu.VMEM((SEQ, CAP, BLK, queries.shape[1]), queries.dtype),
        in_specs=[smem(), vmem()],
        out_specs=vmem(),
        scratch_shapes=[pltpu.SMEM((SEQ,), jnp.int32)],
        compiler_params=SMALL,
        name="dispatch",
    )(owners, queries)


def collect_kernel(owner_ref, c_ref, out_ref, used):
    core = lax.axis_index("core")
    first = (lax.axis_index(SEQ_AXES) - core) * BLOCKS_DEV
    for part in range(2):
        which = jnp.bitwise_xor(core, part)
        for o in range(SEQ):
            used[o] = 0

        def place(b, carry):
            o = owner_ref[first + which * BLOCKS_DEV + b]
            r = used[o]
            used[o] = r + 1
            row = pl.multiple_of((part * BLOCKS_DEV + b) * BLK, BLK)
            out_ref[pl.ds(row, BLK), :] = c_ref[o, which * CAP + r]
            return carry

        lax.fori_loop(0, BLOCKS_DEV, place, 0)


def collect(owners, returned):
    rows = 2 * BLOCKS_DEV * BLK
    return pl.pallas_call(
        collect_kernel,
        out_shape=pltpu.VMEM((rows, returned.shape[-1]), returned.dtype),
        in_specs=[smem(), vmem()],
        out_specs=vmem(),
        scratch_shapes=[pltpu.SMEM((SEQ,), jnp.int32)],
        compiler_params=SMALL,
        name="collect",
    )(owners, *near(returned))


def attend_kernel(late, order, first, meta, q_ref, *refs):
    if late:
        kv_s, _, o_ref, q_s, m_s, acc = refs
    else:
        kv_ref, o_ref, kv_s, q_keep, q_s, m_s, acc = refs
        kv_s[:, :HEAD_DIM] = kv_ref[0, 0]
        kv_s[:, HEAD_DIM : 2 * HEAD_DIM] = kv_ref[0, 1]
        kv_s[:, 2 * HEAD_DIM :] = jnp.ones((KEY_CAP, HEAD_DIM), jnp.bfloat16)
        q_keep[...] = q_ref[...]
    groups = lax.shift_right_logical(meta[0] + GROUP - 1, 3)
    middle = lax.shift_right_logical(groups + 1, 1)
    tiles = meta[1]
    rows = GROUP * HEADS_DEV * BLK
    slot_rows = HEADS_DEV * BLK
    col = lax.broadcasted_iota(jnp.int32, (SUB, HEAD_DIM), 1)

    def group(g, carry):
        for i in range(GROUP):
            slot = order[g * GROUP + i]
            for h in range(HEADS_DEV):
                at = i * slot_rows + h * BLK
                q_s[at : at + BLK, :] = q_ref[slot, :, h * HEAD_DIM : (h + 1) * HEAD_DIM]
        m_s[...] = jnp.full_like(m_s, LOW)
        acc[...] = jnp.zeros_like(acc)

        def tile(t, inner):
            base = pl.multiple_of(t * TILE_STEP, BLK)
            keys = kv_s[pl.ds(base, KEY_BLK), :HEAD_DIM]
            for u in range(rows // SUB):
                part = slice(u * SUB, (u + 1) * SUB)
                s = lax.dot_general(
                    q_s[part, :],
                    keys,
                    (((1,), (1,)), ((), ())),
                    preferred_element_type=jnp.float32,
                )
                tail = KEY_BLK - HEAD_DIM
                head_cols = jnp.where(col >= t, s[:, :HEAD_DIM], LOW)
                tail_cols = jnp.where(col + tail < t + TILE_TOK, s[:, tail:], LOW)
                s = jnp.concatenate([head_cols, s[:, HEAD_DIM:tail], tail_cols], axis=1)
                old = m_s[part, :1]
                new = jnp.maximum(old, jnp.max(s, axis=1, keepdims=True))
                kept, shifts = [], []
                for i in range(SUB // slot_rows):
                    seen = first[g * GROUP + u * (SUB // slot_rows) + i] <= t
                    cut = slice(i * slot_rows, (i + 1) * slot_rows)
                    kept.append(jnp.where(seen, new[cut], old[cut]))
                    shifts.append(jnp.where(seen, new[cut], HIGH))
                new = jnp.concatenate(kept, axis=0)
                high = jnp.concatenate(shifts, axis=0)
                probs = jnp.exp2((s - high) * EXP2_SCALE).astype(jnp.bfloat16)
                fade = jnp.exp2((old - new) * EXP2_SCALE)
                m_s[part, :] = jnp.broadcast_to(new, (SUB, HEAD_DIM))
                acc[part, :] = acc[part, :] * fade + jnp.dot(
                    probs,
                    kv_s[pl.ds(base, KEY_BLK), HEAD_DIM:],
                    preferred_element_type=jnp.float32,
                )
            return inner

        lax.fori_loop(first[g * GROUP], tiles, tile, 0)
        for i in range(GROUP):
            slot = order[g * GROUP + i]
            chip = lax.shift_right_logical(slot, 2)
            place = jnp.bitwise_and(slot, 3)
            for h in range(HEADS_DEV):
                at = i * slot_rows + h * BLK
                cut = slice(at, at + BLK)
                half, inside = divmod(h, HEADS_DEV // 2)
                o_ref[chip, half, place, :, inside * HEAD_DIM : (inside + 1) * HEAD_DIM] = (
                    acc[cut, :HEAD_DIM] / acc[cut, HEAD_DIM:]
                ).astype(jnp.bfloat16)
        return carry

    if late:
        lax.fori_loop(middle, groups, group, 0)
    else:
        lax.fori_loop(0, middle, group, 0)


def attend(order, first, meta, received=None, image_kv=None, earlier=None):
    rows = GROUP * HEADS_DEV * BLK
    late = earlier is not None
    out = pltpu.VMEM((SEQ // 2, 2, 2 * CAP, BLK, HEADS_DEV * HEAD_DIM // 2), jnp.bfloat16)
    if late:
        context, keys, slots = near(*earlier)
        operands = (slots, keys, context)
    else:
        operands = (*near(received), image_kv)
        keys = pltpu.VMEM((KEY_CAP, 3 * HEAD_DIM), jnp.bfloat16)
        slots = pltpu.VMEM(received.shape, received.dtype)
    return pl.pallas_call(
        functools.partial(attend_kernel, late),
        out_shape=out if late else (out, keys, slots),
        input_output_aliases={5: 0} if late else {},
        in_specs=[smem()] * 3 + [vmem()] * len(operands),
        out_specs=vmem() if late else (vmem(),) * 3,
        scratch_shapes=[
            pltpu.VMEM((rows, HEAD_DIM), jnp.bfloat16),
            pltpu.VMEM((rows, HEAD_DIM), jnp.float32),
            pltpu.VMEM((rows, 2 * HEAD_DIM), jnp.float32),
        ],
        compiler_params=LIMIT,
        cost_estimate=pl.CostEstimate(flops=10**10, transcendentals=10**7, bytes_accessed=10**7),
        name="attend_late" if late else "attend_early",
    )(order, first, meta, *operands)


def assemble_kernel(*refs):
    pieces, out_ref = refs[:-1], refs[-1]
    xl = lax.axis_index("xl")
    y = lax.axis_index("y")
    n = 0
    for col in range(2):
        for dy in (0, 3, 1, 2):
            at = jnp.bitwise_xor(xl, col) * 4 + jnp.bitwise_and(y + dy, 3)
            row = 0
            while row < 512:
                size = pieces[n].shape[0]
                out_ref[at, row : row + size, :] = pieces[n][...]
                row += size
                n += 1


def assemble(pieces):
    return pl.pallas_call(
        assemble_kernel,
        out_shape=pltpu.VMEM((8,) + (512, pieces[0].shape[1]), pieces[0].dtype),
        in_specs=[vmem()] * len(pieces),
        out_specs=vmem(),
        compiler_params=SMALL,
        name="assemble",
    )(*near(*pieces))


def weight_spot(dz, flip):
    z = jnp.bitwise_and(lax.axis_index("z") + dz, 3)
    return z * 2 + jnp.bitwise_xor(lax.axis_index("xh"), flip)


def project_first_kernel(own, below, above, across, w, out_ref):
    total = None
    for block, dz, flip in ((own, 0, 0), (below, 3, 0), (above, 1, 0), (across, 0, 1)):
        term = jnp.dot(block[...], w[weight_spot(dz, flip)], preferred_element_type=jnp.float32)
        total = term if total is None else total + term
    out_ref[...] = total


def project_first(own, below, above, across, weights):
    return pl.pallas_call(
        project_first_kernel,
        out_shape=pltpu.VMEM((own.shape[0], weights.shape[2]), jnp.float32),
        in_specs=[vmem()] * 5,
        out_specs=vmem(),
        compiler_params=LIMIT,
        name="project_first",
    )(*near(own, below, above, across, weights))


def project_last_kernel(below, above, far_a, far_b, over_a, over_b, w, total, keep_ref, give_ref):
    half = keep_ref.shape[0]
    full = total[...]
    far = jnp.concatenate([far_a[...], far_b[...]], axis=0)
    over = jnp.concatenate([over_a[...], over_b[...]], axis=0)
    for block, dz, flip in ((below[...], 3, 1), (above[...], 1, 1), (far, 2, 0), (over, 2, 1)):
        full += jnp.dot(block, w[weight_spot(dz, flip)], preferred_element_type=jnp.float32)
    keep_ref[...] = full[:half]
    give_ref[...] = full[half:]


def project_last(blocks, weights, total):
    shape = pltpu.VMEM((total.shape[0] // 2, total.shape[1]), jnp.float32)
    return pl.pallas_call(
        project_last_kernel,
        out_shape=(shape, shape),
        in_specs=[vmem()] * 8,
        out_specs=(vmem(), vmem()),
        compiler_params=LIMIT,
        name="project_last",
    )(*near(*blocks, weights, total))


def routing(owners, starts, here):
    owner_table = owners.reshape(SEQ, BLOCKS_DEV)
    start_table = starts.reshape(SEQ, BLOCKS_DEV)
    ids = jnp.arange(BLOCKS_DEV)
    arriving = owner_table == here
    earlier = ids[None, :] < ids[:, None]
    rank = jnp.sum((arriving[:, None, :] & earlier[None, :, :]).astype(jnp.int32), axis=2)
    hit = arriving[:, None, :] & (rank[:, None, :] == jnp.arange(CAP)[None, :, None])
    slot_start = jnp.sum(jnp.where(hit, start_table[:, None, :], 0), axis=2).reshape(SLOTS)
    active = jnp.any(hit, axis=2).reshape(SLOTS)
    slots = jnp.arange(SLOTS)
    key = jnp.where(active, slot_start, 8) * SLOTS + slots
    position = jnp.sum((key[None, :] < key[:, None]).astype(jnp.int32), axis=1)
    at = position[None, :] == slots[:, None]
    order = jnp.sum(jnp.where(at, slots[None, :], 0), axis=1)
    first = jnp.sum(jnp.where(at, slot_start[None, :], 0), axis=1)
    return order, first, jnp.sum(active.astype(jnp.int32))


def local(
    hidden_in,
    queries,
    image_kv,
    out_weight,
    gate,
    tile_counts,
    owners,
    starts,
    norm_gain,
    norm_grad,
    stream_grad,
):
    here = lax.axis_index(SEQ_AXES)
    width = queries.shape[1]
    half = out_weight.shape[0] // 2

    w = out_weight
    outgoing = dispatch(owners, queries)
    received = lax.all_to_all(outgoing, SEQ_AXES, split_axis=0, concat_axis=0, tiled=True)

    w_lo = lax.ppermute(w, "y", UP)
    w_hi = lax.ppermute(w, "y", DOWN)
    w_x = lax.ppermute(w, "xl", SWAP)

    order, first, n_active = routing(owners, starts, here)
    tiles = lax.dynamic_index_in_dim(tile_counts, here, 0, keepdims=False)
    meta = jnp.stack([n_active, tiles])
    slots = received.reshape(SLOTS, BLK, width)
    early = attend(order, first, meta, slots, image_kv)

    far_a = lax.ppermute(w_lo[:half], "y", UP)
    far_b = lax.ppermute(w_hi[half:], "y", DOWN)
    x_lo_a = lax.ppermute(w_x[:half], "y", UP)
    x_hi_a = lax.ppermute(w_x[:half], "y", DOWN)
    x_lo_b = lax.ppermute(w_lo[half:], "xl", SWAP)
    x_hi_b = lax.ppermute(w_hi[half:], "xl", SWAP)

    context = attend(order, first, meta, earlier=early)

    x_far_a = lax.ppermute(x_lo_a, "y", UP)
    x_far_b = lax.ppermute(far_b, "xl", SWAP)

    context = context.reshape(SEQ, 2 * CAP, BLK, width // 2)
    returned = lax.all_to_all(context, SEQ_AXES, split_axis=0, concat_axis=0, tiled=True)
    weights = assemble(
        (w, w_lo, w_hi, far_a, far_b)
        + (w_x, x_lo_a, x_lo_b, x_hi_a, x_hi_b, x_far_a, x_far_b)
    )
    own = collect(owners, returned)
    below = lax.ppermute(own, "z", UP)
    above = lax.ppermute(own, "z", DOWN)
    across = lax.ppermute(own, "xh", SWAP)
    rows = own.shape[0] // 2
    far_a = lax.ppermute(below[:rows], "z", UP)
    far_b = lax.ppermute(above[rows:], "z", DOWN)
    across_below = lax.ppermute(across, "z", UP)
    across_above = lax.ppermute(across, "z", DOWN)
    over_a = lax.ppermute(far_a, "xh", SWAP)
    over_b = lax.ppermute(far_b, "xh", SWAP)
    total = project_first(own, below, above, across, weights)
    blocks = (across_below, across_above, far_a, far_b, over_a, over_b)
    keep, give = project_last(blocks, weights, total)
    branch = keep + lax.ppermute(give, "core", SWAP)

    hidden_out = (hidden_in.astype(jnp.float32) + jnp.tanh(gate[0]) * branch).astype(jnp.bfloat16)
    hidden = hidden_out.astype(jnp.float32)
    scaled = norm_gain[None, :] * norm_grad.astype(jnp.float32)
    sums = jnp.stack([jnp.sum(hidden * hidden, axis=1), jnp.sum(hidden * scaled, axis=1)])
    copies = jnp.broadcast_to(sums[None], (8,) + sums.shape)
    copies = lax.all_to_all(copies, HEAD_AXES, split_axis=0, concat_axis=0, tiled=True)
    squares, product = jnp.sum(copies, axis=0)
    inverse = lax.rsqrt(squares / D + EPS)[:, None]
    project_mean = (product / D)[:, None]
    stream_in_grad = (
        stream_grad.astype(jnp.float32) + inverse * scaled - inverse**3 * project_mean * hidden
    )
    return (hidden_out, stream_in_grad)


def solution(mesh):
    fine = Mesh(mesh.devices.reshape(2, 4, 2, 4, 2), SEQ_AXES + HEAD_AXES)
    both = P(SEQ_AXES, HEAD_AXES)
    placed = (
        both,
        both,
        P(SEQ_AXES, None, None, HEAD_AXES),
        both,
        P(),
        P(),
        P(),
        P(),
        P(HEAD_AXES),
        both,
        both,
    )
    return jax.shard_map(
        local,
        mesh=fine,
        in_specs=placed,
        out_specs=(both, both),
        check_vma=False,
    )
```

profile of v0, /device:TPU:0, one launch (start us, length us, event | category | flops | bytes accessed | tf_op | source)
XLA Modules:
  0.0 179.1 jit_solution(1635287462773353780)
XLA Ops:
  0.6 3.2 %collective-permute-start.10 = (bf16[512,1024]{1,0:T(8,128)(2,1)}, bf16[512,1024]{1,0:T(8,128)(2,1)S(1)}, u32[]{:S(2)}, u32[]{:S(2)}) collective-permute-start(bf16[512,1024]{1,0:T(8,128)(2,1)} %refs_0_.3), channel_id=1, source_target_pairs={{0,48},{16,0},{32,16},{48,32},{1,49},{17,1},{33,17},{49,33},{2,50}... | collective-permute-start | bytes 3145736 | tf_op jit(solution)/shard_map/ppermute | solution.py:337
  3.8 1.5 collective-permute-start.13
  5.3 1.0 copy-done.2
  6.4 0.7 copy-done.3
  7.0 1.7 dispatch.1
  8.8 4.6 %all-to-all-start = ((bf16[16,2,16,1024]{3,2,1,0:T(8,128)(2,1)}), bf16[16,2,16,1024]{3,2,1,0:T(8,128)(2,1)S(1)}, u32[]{:S(2)}, u32[]{:S(2)}) async-start(bf16[16,2,16,1024]{3,2,1,0:T(8,128)(2,1)} %dispatch.1), calls=%async_computation | async-start | bytes 2097152 | tf_op jit(solution)/shard_map/all_to_all | solution.py:334
  13.4 0.7 broadcast_compare_fusion
  14.9 0.8 broadcast_in_dim.57
  15.9 1.2 dynamic_slice.4
  17.2 0.7 convert_reduce_fusion.2
  17.9 1.4 pad_add_fusion.meta
  19.6 22.7 %all-to-all-done = bf16[16,2,16,1024]{3,2,1,0:T(8,128)(2,1)S(1)} async-done(((bf16[16,2,16,1024]{3,2,1,0:T(8,128)(2,1)}), bf16[16,2,16,1024]{3,2,1,0:T(8,128)(2,1)S(1)}, u32[]{:S(2)}, u32[]{:S(2)}) %all-to-all-start) | async-done | bytes 1048608 | tf_op jit(solution)/shard_map/all_to_all | solution.py:334
  42.3 1.9 %copy-done.5 = bf16[1,2,6528,128]{3,2,1,0:T(8,128)(2,1)S(1)} copy-done((bf16[1,2,6528,128]{3,2,1,0:T(8,128)(2,1)S(1)}, bf16[1,2,6528,128]{3,2,1,0:T(8,128)(2,1)}, u32[]{:S(2)}) %copy-start.5) | copy-done | bytes 3342360
  44.2 18.7 %attend_early.1 = (bf16[8,2,4,16,512]{4,3,2,1,0:T(8,128)(2,1)S(1)}, bf16[6528,384]{1,0:T(8,128)(2,1)S(1)}, bf16[32,16,1024]{2,1,0:T(8,128)(2,1)S(1)}) custom-call(s32[32]{0:T(128)S(1)} %get-tuple-element.15.order, s32[32]{0:T(128)S(1)} %get-tuple-element.14.first, s32[2]{0:T(128)S(1)} %pad_add_fusion.meta, bf16[32,16,1024]{2,1,0:T(8,128)(2,1)S(1)} %bitcast.8, ...), custom_call_target="tpu_custom_call" | custom-call | flops 10000000000 | bytes 10000000 | tf_op jit(solution)/shard_map/attend_early/pallas_call | solution.py:205
  63.0 10.6 %attend_late.1 = bf16[8,2,4,16,512]{4,3,2,1,0:T(8,128)(2,1)S(1)} custom-call(s32[32]{0:T(128)S(1)} %get-tuple-element.15.order, s32[32]{0:T(128)S(1)} %get-tuple-element.14.first, s32[2]{0:T(128)S(1)} %pad_add_fusion.meta, bf16[32,16,1024]{2,1,0:T(8,128)(2,1)S(1)} %get-tuple-element.7.q_ref, ...), custom_call_target="tpu_custom_call", output_to_operand_aliasing={{}: (5, {})} | custom-call | flops 10000000000 | bytes 10000000 | tf_op jit(solution)/shard_map/attend_late/pallas_call | solution.py:205
  73.6 1.0 copy-done.1
  74.6 3.8 %all-to-all-start.1 = ((bf16[16,4,16,512]{3,2,1,0:T(8,128)(2,1)}), bf16[16,4,16,512]{3,2,1,0:T(8,128)(2,1)S(1)}, u32[]{:S(2)}, u32[]{:S(2)}) async-start(bf16[16,4,16,512]{3,2,1,0:T(8,128)(2,1)} %bitcast.9), calls=%async_computation.1 | async-start | bytes 2097152 | tf_op jit(solution)/shard_map/all_to_all | solution.py:359
  78.4 0.8 slice.29
  79.3 1.8 %collective-permute-start.17 = (bf16[256,1024]{1,0:T(8,128)(2,1)}, bf16[256,1024]{1,0:T(8,128)(2,1)}, u32[]{:S(2)}, u32[]{:S(2)}) collective-permute-start(bf16[256,1024]{1,0:T(8,128)(2,1)} %slice.29), channel_id=1, source_target_pairs={{0,64},{64,0},{1,65},{65,1},{2,66},{66,2},{3,67},{67,3},{4,68},{68... | collective-permute-start | bytes 1572872 | tf_op jit(solution)/shard_map/ppermute | solution.py:351
  81.1 2.7 %collective-permute-start.12 = (bf16[256,1024]{1,0:T(8,128)(2,1)}, bf16[256,1024]{1,0:T(8,128)(2,1)}, u32[]{:S(2)}, u32[]{:S(2)}) collective-permute-start(bf16[256,1024]{1,0:T(8,128)(2,1)} %slice.29), channel_id=1, source_target_pairs={{0,48},{16,0},{32,16},{48,32},{1,49},{17,1},{33,17},{49,33},{2,50}... | collective-permute-start | bytes 1572872 | tf_op jit(solution)/shard_map/ppermute | solution.py:347
  83.8 1.1 fusion.8
  84.9 0.5 collective-permute-start.15
  85.4 10.1 %all-to-all-done.1.c_ref = bf16[16,4,16,512]{3,2,1,0:T(8,128)(2,1)S(1)} async-done(((bf16[16,4,16,512]{3,2,1,0:T(8,128)(2,1)}), bf16[16,4,16,512]{3,2,1,0:T(8,128)(2,1)S(1)}, u32[]{:S(2)}, u32[]{:S(2)}) %all-to-all-start.1) | async-done | bytes 1048608 | tf_op jit(solution)/shard_map/all_to_all | solution.py:359
  95.5 1.0 collect.1.own
  96.5 4.1 %collective-permute-start.5 = (bf16[512,512]{1,0:T(8,128)(2,1)S(1)}, bf16[512,512]{1,0:T(8,128)(2,1)S(1)}, u32[]{:S(2)}, u32[]{:S(2)}) collective-permute-start(bf16[512,512]{1,0:T(8,128)(2,1)S(1)} %collect.1.own), channel_id=1, source_target_pairs={{0,6},{2,0},{4,2},{6,4},{1,7},{3,1},{5,3},{7,5},{8,14},{10,8},{12,... | collective-permute-start | bytes 1572872 | tf_op jit(solution)/shard_map/ppermute | solution.py:366
  100.6 1.1 slice.30
  101.7 3.0 %collective-permute-done.17.refs_9_ = bf16[256,1024]{1,0:T(8,128)(2,1)} collective-permute-done((bf16[256,1024]{1,0:T(8,128)(2,1)}, bf16[256,1024]{1,0:T(8,128)(2,1)}, u32[]{:S(2)}, u32[]{:S(2)}) %collective-permute-start.17) | collective-permute-done | bytes 524320 | tf_op jit(solution)/shard_map/ppermute | solution.py:351
  104.7 1.5 collective-permute-start.14
  106.1 1.4 collective-permute-start.11
  107.6 7.8 %collective-permute-done.15.refs_7_ = bf16[256,1024]{1,0:T(8,128)(2,1)} collective-permute-done((bf16[256,1024]{1,0:T(8,128)(2,1)}, bf16[256,1024]{1,0:T(8,128)(2,1)}, u32[]{:S(2)}, u32[]{:S(2)}) %collective-permute-start.15) | collective-permute-done | bytes 524320 | tf_op jit(solution)/shard_map/ppermute | solution.py:350
  115.3 2.7 %collective-permute-start.16 = (bf16[256,1024]{1,0:T(8,128)(2,1)S(1)}, bf16[256,1024]{1,0:T(8,128)(2,1)S(1)}, u32[]{:S(2)}, u32[]{:S(2)}) collective-permute-start(bf16[256,1024]{1,0:T(8,128)(2,1)S(1)} %slice.30), channel_id=1, source_target_pairs={{0,48},{16,0},{32,16},{48,32},{1,49},{17,1},{33,17},{49,33},{2,50}... | collective-permute-start | bytes 1572872 | tf_op jit(solution)/shard_map/ppermute | solution.py:349
  118.0 3.0 %collective-permute-start = (bf16[512,512]{1,0:T(8,128)(2,1)S(1)}, bf16[512,512]{1,0:T(8,128)(2,1)S(1)}, u32[]{:S(2)}, u32[]{:S(2)}) collective-permute-start(bf16[512,512]{1,0:T(8,128)(2,1)S(1)} %collect.1.own), channel_id=1, source_target_pairs={{0,1},{1,0},{2,3},{3,2},{4,5},{5,4},{6,7},{7,6},{8,9},{9,8},{10,11... | collective-permute-start | bytes 1572872 | tf_op jit(solution)/shard_map/ppermute | solution.py:367
  121.2 10.7 %collective-permute-done.11.refs_3_ = bf16[256,1024]{1,0:T(8,128)(2,1)S(1)} collective-permute-done((bf16[256,1024]{1,0:T(8,128)(2,1)}, bf16[256,1024]{1,0:T(8,128)(2,1)S(1)}, u32[]{:S(2)}, u32[]{:S(2)}) %collective-permute-start.11) | collective-permute-done | bytes 524320 | tf_op jit(solution)/shard_map/ppermute | solution.py:346
  131.9 4.0 %collective-permute-start.6 = (bf16[256,512]{1,0:T(8,128)(2,1)S(1)}, bf16[256,512]{1,0:T(8,128)(2,1)S(1)}, u32[]{:S(2)}, u32[]{:S(2)}) collective-permute-start(bf16[256,512]{1,0:T(8,128)(2,1)S(1)} %slice.27), channel_id=1, source_target_pairs={{0,6},{2,0},{4,2},{6,4},{1,7},{3,1},{5,3},{7,5},{8,14},{10,8},{12,... | collective-permute-start | bytes 786440 | tf_op jit(solution)/shard_map/ppermute | solution.py:370
  136.0 3.2 %collective-permute-start.2 = (bf16[512,512]{1,0:T(8,128)(2,1)S(1)}, bf16[512,512]{1,0:T(8,128)(2,1)S(1)}, u32[]{:S(2)}, u32[]{:S(2)}) collective-permute-start(bf16[512,512]{1,0:T(8,128)(2,1)S(1)} %collective-permute-done.across), channel_id=1, source_target_pairs={{0,6},{2,0},{4,2},{6,4},{1,7},{3,1},{5,3},{7,5},{8,14},{10,8},{12,... | collective-permute-start | bytes 1572872 | tf_op jit(solution)/shard_map/ppermute | solution.py:372
  139.2 4.1 %collective-permute-done.19.refs_11_ = bf16[256,1024]{1,0:T(8,128)(2,1)S(1)} collective-permute-done((bf16[256,1024]{1,0:T(8,128)(2,1)}, bf16[256,1024]{1,0:T(8,128)(2,1)S(1)}, u32[]{:S(2)}, u32[]{:S(2)}) %collective-permute-start.19) | collective-permute-done | bytes 524320 | tf_op jit(solution)/shard_map/ppermute | solution.py:356
  143.3 1.9 %collective-permute-start.1 = (bf16[512,512]{1,0:T(8,128)(2,1)S(1)}, bf16[512,512]{1,0:T(8,128)(2,1)S(1)}, u32[]{:S(2)}, u32[]{:S(2)}) collective-permute-start(bf16[512,512]{1,0:T(8,128)(2,1)S(1)} %collective-permute-done.across), channel_id=1, source_target_pairs={{0,2},{2,4},{4,6},{6,0},{1,3},{3,5},{5,7},{7,1},{8,10},{10,12},{12... | collective-permute-start | bytes 1572872 | tf_op jit(solution)/shard_map/ppermute | solution.py:371
  145.2 1.7 collective-permute-start.8
  146.9 1.8 %collective-permute-start.7 = (bf16[256,512]{1,0:T(8,128)(2,1)S(1)}, bf16[256,512]{1,0:T(8,128)(2,1)S(1)}, u32[]{:S(2)}, u32[]{:S(2)}) collective-permute-start(bf16[256,512]{1,0:T(8,128)(2,1)S(1)} %collective-permute-done.4.far_a), channel_id=1, source_target_pairs={{0,1},{1,0},{2,3},{3,2},{4,5},{5,4},{6,7},{7,6},{8,9},{9,8},{10,11... | collective-permute-start | bytes 786440 | tf_op jit(solution)/shard_map/ppermute | solution.py:373
  148.7 1.2 copy-done
  150.0 2.2 %assemble.1.w = bf16[8,512,1024]{2,1,0:T(8,128)(2,1)S(1)} custom-call(bf16[512,1024]{1,0:T(8,128)(2,1)S(1)} %copy-done, bf16[512,1024]{1,0:T(8,128)(2,1)S(1)} %collective-permute-done.9.refs_1_, bf16[512,1024]{1,0:T(8,128)(2,1)S(1)} %collective-permute-done.10.refs_2_, bf16[256,1024]{1,0:T(8,128)(2,1)S(1)} %collective-permute-done.11.refs_3_, ...), custom_call_target="tpu_custom_call" | custom-call | tf_op jit(solution)/shard_map/assemble/pallas_call | solution.py:239
  152.2 2.3 %project_first.1.total = f32[512,1024]{1,0:T(8,128)S(1)} custom-call(bf16[512,512]{1,0:T(8,128)(2,1)S(1)} %collect.1.own, bf16[512,512]{1,0:T(8,128)(2,1)S(1)} %collective-permute-done.3.below, bf16[512,512]{1,0:T(8,128)(2,1)S(1)} %collective-permute-done.5.above, bf16[512,512]{1,0:T(8,128)(2,1)S(1)} %collective-permute-done.across, ...), custom_call_target="tpu_custom_call" | custom-call | tf_op jit(solution)/shard_map/project_first/pallas_call | solution.py:263
  154.6 1.3 collective-permute-done.8.over_b
  155.9 2.8 %collective-permute-done.7.over_a = bf16[256,512]{1,0:T(8,128)(2,1)S(1)} collective-permute-done((bf16[256,512]{1,0:T(8,128)(2,1)S(1)}, bf16[256,512]{1,0:T(8,128)(2,1)S(1)}, u32[]{:S(2)}, u32[]{:S(2)}) %collective-permute-start.7) | collective-permute-done | bytes 262176 | tf_op jit(solution)/shard_map/ppermute | solution.py:373
  158.7 2.3 %project_last.1 = (f32[256,1024]{1,0:T(8,128)S(1)}, f32[256,1024]{1,0:T(8,128)S(1)}) custom-call(bf16[512,512]{1,0:T(8,128)(2,1)S(1)} %collective-permute-done.1.below, bf16[512,512]{1,0:T(8,128)(2,1)S(1)} %collective-permute-done.2.above, bf16[256,512]{1,0:T(8,128)(2,1)S(1)} %collective-permute-done.4.far_a, ...), custom_call_target="tpu_custom_call" | custom-call | tf_op jit(solution)/shard_map/project_last/pallas_call | solution.py:286
  161.8 2.0 %collective-permute-done.20 = f32[256,1024]{1,0:T(8,128)S(1)} collective-permute-done((f32[256,1024]{1,0:T(8,128)S(1)}, f32[256,1024]{1,0:T(8,128)S(1)}, u32[]{:S(2)}, u32[]{:S(2)}) %collective-permute-start.20) | collective-permute-done | bytes 1048608 | tf_op jit(solution)/shard_map/ppermute | solution.py:378
  164.3 13.5 %all_to_all.15 = f32[8,2,256]{2,1,0:T(2,128)S(1)} all-to-all(f32[8,2,256]{2,1,0:T(2,128)S(1)} %broadcast_in_dim.64), channel_id=1, replica_groups=mesh['xl'=2,'y'=4,'core'=2,'z'=4,'xh'=2] {'z','xh'}, dimensions={0} | all-to-all | bytes 32768 | tf_op jit(solution)/shard_map/all_to_all | solution.py:385
  177.8 1.3 fusion.2
  (57 shorter events, 2.2 us)
Async XLA Ops:
  0.6 77.8 %collective-permute-start.10 = (bf16[512,1024]{1,0:T(8,128)(2,1)}, bf16[512,1024]{1,0:T(8,128)(2,1)S(1)}, u32[]{:S(2)}, u32[]{:S(2)}) collective-permute-start(bf16[512,1024]{1,0:T(8,128)(2,1)} %refs_0_.3), channel_id=1, source_target_pairs={{0,48},{16,0},{32,16},{48,32},{1,49},{17,1},{33,17},{49,33},{2,50}... | collective-permute-start | bytes 3145736 | tf_op jit(solution)/shard_map/ppermute | solution.py:337
  3.8 80.0 %collective-permute-start.9 = (bf16[512,1024]{1,0:T(8,128)(2,1)}, bf16[512,1024]{1,0:T(8,128)(2,1)S(1)}, u32[]{:S(2)}, u32[]{:S(2)}) collective-permute-start(bf16[512,1024]{1,0:T(8,128)(2,1)} %refs_0_.3), channel_id=1, source_target_pairs={{0,16},{16,32},{32,48},{48,0},{1,17},{17,33},{33,49},{49,1},{2,18}... | collective-permute-start | bytes 3145736 | tf_op jit(solution)/shard_map/ppermute | solution.py:336
  3.8 96.7 %collective-permute-start.13 = (bf16[512,1024]{1,0:T(8,128)(2,1)}, bf16[512,1024]{1,0:T(8,128)(2,1)}, u32[]{:S(2)}, u32[]{:S(2)}) collective-permute-start(bf16[512,1024]{1,0:T(8,128)(2,1)} %refs_0_.3), channel_id=1, source_target_pairs={{0,64},{64,0},{1,65},{65,1},{2,66},{66,2},{3,67},{67,3},{4,68},{68... | collective-permute-start | bytes 3145736 | tf_op jit(solution)/shard_map/ppermute | solution.py:338
  5.3 1.0 copy-start.2
  6.4 0.7 copy-start.3
  8.8 33.5 %all-to-all-start = ((bf16[16,2,16,1024]{3,2,1,0:T(8,128)(2,1)}), bf16[16,2,16,1024]{3,2,1,0:T(8,128)(2,1)S(1)}, u32[]{:S(2)}, u32[]{:S(2)}) async-start(bf16[16,2,16,1024]{3,2,1,0:T(8,128)(2,1)} %dispatch.1), calls=%async_computation | async-start | bytes 2097152 | tf_op jit(solution)/shard_map/all_to_all | solution.py:334
  42.3 1.9 %copy-start.5 = (bf16[1,2,6528,128]{3,2,1,0:T(8,128)(2,1)S(1)}, bf16[1,2,6528,128]{3,2,1,0:T(8,128)(2,1)}, u32[]{:S(2)}) copy-start(bf16[1,2,6528,128]{3,2,1,0:T(8,128)(2,1)} %refs_0_.2) | copy-start | bytes 10027012
  73.6 1.0 copy-start.1
  74.6 20.9 %copy-start.4 = (s32[256]{0:T(256)S(1)}, s32[256]{0:T(256)}, u32[]{:S(2)}) copy-start(s32[256]{0:T(256)} %owner_ref.3) | copy-start | bytes 3076
  74.6 20.9 %all-to-all-start.1 = ((bf16[16,4,16,512]{3,2,1,0:T(8,128)(2,1)}), bf16[16,4,16,512]{3,2,1,0:T(8,128)(2,1)S(1)}, u32[]{:S(2)}, u32[]{:S(2)}) async-start(bf16[16,4,16,512]{3,2,1,0:T(8,128)(2,1)} %bitcast.9), calls=%async_computation.1 | async-start | bytes 2097152 | tf_op jit(solution)/shard_map/all_to_all | solution.py:359
  79.3 25.4 %collective-permute-start.17 = (bf16[256,1024]{1,0:T(8,128)(2,1)}, bf16[256,1024]{1,0:T(8,128)(2,1)}, u32[]{:S(2)}, u32[]{:S(2)}) collective-permute-start(bf16[256,1024]{1,0:T(8,128)(2,1)} %slice.29), channel_id=1, source_target_pairs={{0,64},{64,0},{1,65},{65,1},{2,66},{66,2},{3,67},{67,3},{4,68},{68... | collective-permute-start | bytes 1572872 | tf_op jit(solution)/shard_map/ppermute | solution.py:351
  81.1 25.0 %collective-permute-start.12 = (bf16[256,1024]{1,0:T(8,128)(2,1)}, bf16[256,1024]{1,0:T(8,128)(2,1)}, u32[]{:S(2)}, u32[]{:S(2)}) collective-permute-start(bf16[256,1024]{1,0:T(8,128)(2,1)} %slice.29), channel_id=1, source_target_pairs={{0,48},{16,0},{32,16},{48,32},{1,49},{17,1},{33,17},{49,33},{2,50}... | collective-permute-start | bytes 1572872 | tf_op jit(solution)/shard_map/ppermute | solution.py:347
  84.9 30.4 %collective-permute-start.15 = (bf16[256,1024]{1,0:T(8,128)(2,1)}, bf16[256,1024]{1,0:T(8,128)(2,1)}, u32[]{:S(2)}, u32[]{:S(2)}) collective-permute-start(bf16[256,1024]{1,0:T(8,128)(2,1)} %get-tuple-element.17), channel_id=1, source_target_pairs={{0,64},{64,0},{1,65},{65,1},{2,66},{66,2},{3,67},{67,3},{4,68},{68... | collective-permute-start | bytes 1572872 | tf_op jit(solution)/shard_map/ppermute | solution.py:350
  96.5 21.6 %collective-permute-start.5 = (bf16[512,512]{1,0:T(8,128)(2,1)S(1)}, bf16[512,512]{1,0:T(8,128)(2,1)S(1)}, u32[]{:S(2)}, u32[]{:S(2)}) collective-permute-start(bf16[512,512]{1,0:T(8,128)(2,1)S(1)} %collect.1.own), channel_id=1, source_target_pairs={{0,6},{2,0},{4,2},{6,4},{1,7},{3,1},{5,3},{7,5},{8,14},{10,8},{12,... | collective-permute-start | bytes 1572872 | tf_op jit(solution)/shard_map/ppermute | solution.py:366
  100.6 20.5 %collective-permute-start.3 = (bf16[512,512]{1,0:T(8,128)(2,1)S(1)}, bf16[512,512]{1,0:T(8,128)(2,1)S(1)}, u32[]{:S(2)}, u32[]{:S(2)}) collective-permute-start(bf16[512,512]{1,0:T(8,128)(2,1)S(1)} %collect.1.own), channel_id=1, source_target_pairs={{0,2},{2,4},{4,6},{6,0},{1,3},{3,5},{5,7},{7,1},{8,10},{10,12},{12... | collective-permute-start | bytes 1572872 | tf_op jit(solution)/shard_map/ppermute | solution.py:365
  104.7 16.5 %collective-permute-start.14 = (bf16[256,1024]{1,0:T(8,128)(2,1)S(1)}, bf16[256,1024]{1,0:T(8,128)(2,1)S(1)}, u32[]{:S(2)}, u32[]{:S(2)}) collective-permute-start(bf16[256,1024]{1,0:T(8,128)(2,1)S(1)} %slice.30), channel_id=1, source_target_pairs={{0,16},{16,32},{32,48},{48,0},{1,17},{17,33},{33,49},{49,1},{2,18}... | collective-permute-start | bytes 1572872 | tf_op jit(solution)/shard_map/ppermute | solution.py:348
  106.1 25.7 %collective-permute-start.11 = (bf16[256,1024]{1,0:T(8,128)(2,1)}, bf16[256,1024]{1,0:T(8,128)(2,1)S(1)}, u32[]{:S(2)}, u32[]{:S(2)}) collective-permute-start(bf16[256,1024]{1,0:T(8,128)(2,1)} %get-tuple-element.18), channel_id=1, source_target_pairs={{0,16},{16,32},{32,48},{48,0},{1,17},{17,33},{33,49},{49,1},{2,18}... | collective-permute-start | bytes 1572872 | tf_op jit(solution)/shard_map/ppermute | solution.py:346
  115.3 20.6 %collective-permute-start.16 = (bf16[256,1024]{1,0:T(8,128)(2,1)S(1)}, bf16[256,1024]{1,0:T(8,128)(2,1)S(1)}, u32[]{:S(2)}, u32[]{:S(2)}) collective-permute-start(bf16[256,1024]{1,0:T(8,128)(2,1)S(1)} %slice.30), channel_id=1, source_target_pairs={{0,48},{16,0},{32,16},{48,32},{1,49},{17,1},{33,17},{49,33},{2,50}... | collective-permute-start | bytes 1572872 | tf_op jit(solution)/shard_map/ppermute | solution.py:349
  118.0 17.9 %collective-permute-start = (bf16[512,512]{1,0:T(8,128)(2,1)S(1)}, bf16[512,512]{1,0:T(8,128)(2,1)S(1)}, u32[]{:S(2)}, u32[]{:S(2)}) collective-permute-start(bf16[512,512]{1,0:T(8,128)(2,1)S(1)} %collect.1.own), channel_id=1, source_target_pairs={{0,1},{1,0},{2,3},{3,2},{4,5},{5,4},{6,7},{7,6},{8,9},{9,8},{10,11... | collective-permute-start | bytes 1572872 | tf_op jit(solution)/shard_map/ppermute | solution.py:367
  121.1 22.2 %collective-permute-start.19 = (bf16[256,1024]{1,0:T(8,128)(2,1)}, bf16[256,1024]{1,0:T(8,128)(2,1)S(1)}, u32[]{:S(2)}, u32[]{:S(2)}) collective-permute-start(bf16[256,1024]{1,0:T(8,128)(2,1)} %collective-permute-done.12.refs_4_), channel_id=1, source_target_pairs={{0,64},{64,0},{1,65},{65,1},{2,66},{66,2},{3,67},{67,3},{4,68},{68... | collective-permute-start | bytes 1572872 | tf_op jit(solution)/shard_map/ppermute | solution.py:356
  121.1 27.6 %collective-permute-start.18 = (bf16[256,1024]{1,0:T(8,128)(2,1)S(1)}, bf16[256,1024]{1,0:T(8,128)(2,1)S(1)}, u32[]{:S(2)}, u32[]{:S(2)}) collective-permute-start(bf16[256,1024]{1,0:T(8,128)(2,1)S(1)} %collective-permute-done.14.refs_6_), channel_id=1, source_target_pairs={{0,16},{16,32},{32,48},{48,0},{1,17},{17,33},{33,49},{49,1},{2,18}... | collective-permute-start | bytes 1572872 | tf_op jit(solution)/shard_map/ppermute | solution.py:355
  131.9 13.3 %collective-permute-start.6 = (bf16[256,512]{1,0:T(8,128)(2,1)S(1)}, bf16[256,512]{1,0:T(8,128)(2,1)S(1)}, u32[]{:S(2)}, u32[]{:S(2)}) collective-permute-start(bf16[256,512]{1,0:T(8,128)(2,1)S(1)} %slice.27), channel_id=1, source_target_pairs={{0,6},{2,0},{4,2},{6,4},{1,7},{3,1},{5,3},{7,5},{8,14},{10,8},{12,... | collective-permute-start | bytes 786440 | tf_op jit(solution)/shard_map/ppermute | solution.py:370
  135.9 11.0 %collective-permute-start.4 = (bf16[256,512]{1,0:T(8,128)(2,1)S(1)}, bf16[256,512]{1,0:T(8,128)(2,1)S(1)}, u32[]{:S(2)}, u32[]{:S(2)}) collective-permute-start(bf16[256,512]{1,0:T(8,128)(2,1)S(1)} %slice.26), channel_id=1, source_target_pairs={{0,2},{2,4},{4,6},{6,0},{1,3},{3,5},{5,7},{7,1},{8,10},{10,12},{12... | collective-permute-start | bytes 786440 | tf_op jit(solution)/shard_map/ppermute | solution.py:369
  136.0 22.7 %collective-permute-start.2 = (bf16[512,512]{1,0:T(8,128)(2,1)S(1)}, bf16[512,512]{1,0:T(8,128)(2,1)S(1)}, u32[]{:S(2)}, u32[]{:S(2)}) collective-permute-start(bf16[512,512]{1,0:T(8,128)(2,1)S(1)} %collective-permute-done.across), channel_id=1, source_target_pairs={{0,6},{2,0},{4,2},{6,4},{1,7},{3,1},{5,3},{7,5},{8,14},{10,8},{12,... | collective-permute-start | bytes 1572872 | tf_op jit(solution)/shard_map/ppermute | solution.py:372
  143.3 15.4 %collective-permute-start.1 = (bf16[512,512]{1,0:T(8,128)(2,1)S(1)}, bf16[512,512]{1,0:T(8,128)(2,1)S(1)}, u32[]{:S(2)}, u32[]{:S(2)}) collective-permute-start(bf16[512,512]{1,0:T(8,128)(2,1)S(1)} %collective-permute-done.across), channel_id=1, source_target_pairs={{0,2},{2,4},{4,6},{6,0},{1,3},{3,5},{5,7},{7,1},{8,10},{10,12},{12... | collective-permute-start | bytes 1572872 | tf_op jit(solution)/shard_map/ppermute | solution.py:371
  145.2 10.7 %collective-permute-start.8 = (bf16[256,512]{1,0:T(8,128)(2,1)S(1)}, bf16[256,512]{1,0:T(8,128)(2,1)S(1)}, u32[]{:S(2)}, u32[]{:S(2)}) collective-permute-start(bf16[256,512]{1,0:T(8,128)(2,1)S(1)} %collective-permute-done.6.far_b), channel_id=1, source_target_pairs={{0,1},{1,0},{2,3},{3,2},{4,5},{5,4},{6,7},{7,6},{8,9},{9,8},{10,11... | collective-permute-start | bytes 786440 | tf_op jit(solution)/shard_map/ppermute | solution.py:374
  146.9 11.7 %collective-permute-start.7 = (bf16[256,512]{1,0:T(8,128)(2,1)S(1)}, bf16[256,512]{1,0:T(8,128)(2,1)S(1)}, u32[]{:S(2)}, u32[]{:S(2)}) collective-permute-start(bf16[256,512]{1,0:T(8,128)(2,1)S(1)} %collective-permute-done.4.far_a), channel_id=1, source_target_pairs={{0,1},{1,0},{2,3},{3,2},{4,5},{5,4},{6,7},{7,6},{8,9},{9,8},{10,11... | collective-permute-start | bytes 786440 | tf_op jit(solution)/shard_map/ppermute | solution.py:373
  148.7 1.2 copy-start
  154.5 9.2 %copy-start.6 = (bf16[256,1024]{1,0:T(8,128)(2,1)S(1)}, bf16[256,1024]{1,0:T(8,128)(2,1)}, u32[]{:S(2)}) copy-start(bf16[256,1024]{1,0:T(8,128)(2,1)} %param.20) | copy-start | bytes 1572868
  154.5 9.2 %copy-start.8 = (bf16[256,1024]{1,0:T(8,128)(2,1)S(1)}, bf16[256,1024]{1,0:T(8,128)(2,1)}, u32[]{:S(2)}) copy-start(bf16[256,1024]{1,0:T(8,128)(2,1)} %param.11) | copy-start | bytes 1572868
  154.6 9.2 %copy-start.10 = (f32[1024]{0:T(1024)S(1)}, f32[1024]{0:T(1024)}, u32[]{:S(2)}) copy-start(f32[1024]{0:T(1024)} %param.19) | copy-start | bytes 12292
  154.6 23.3 %copy-start.9 = (bf16[256,1024]{1,0:T(8,128)(2,1)S(1)}, bf16[256,1024]{1,0:T(8,128)(2,1)}, u32[]{:S(2)}) copy-start(bf16[256,1024]{1,0:T(8,128)(2,1)} %param.21) | copy-start | bytes 1572868
  161.0 2.7 %collective-permute-start.20 = (f32[256,1024]{1,0:T(8,128)S(1)}, f32[256,1024]{1,0:T(8,128)S(1)}, u32[]{:S(2)}, u32[]{:S(2)}) collective-permute-start(f32[256,1024]{1,0:T(8,128)S(1)} %get-tuple-element.11), channel_id=1, source_target_pairs={{0,8},{8,0},{1,9},{9,1},{2,10},{10,2},{3,11},{11,3},{4,12},{12,4},... | collective-permute-start | bytes 3145736 | tf_op jit(solution)/shard_map/ppermute | solution.py:378
  164.2 14.9 %copy-start.7 = (bf16[256,1024]{1,0:T(8,128)(2,1)}, bf16[256,1024]{1,0:T(8,128)(2,1)S(1)}, u32[]{:S(2)}) copy-start(bf16[256,1024]{1,0:T(8,128)(2,1)S(1)} %get-tuple-element.16) | copy-start | bytes 1572868
where the time goes:
time: 180 us; the launch traced here: 179 us
  waiting for transfers between devices  64.4 us (36%)
  starting transfers between devices  43.8 us (24%)
  Pallas kernels  39 us (22%)
  blocking collectives  13.5 us (8%)
  local copies, waits for them, and re-layouts  11.4 us (6%)
  other arithmetic  5.49 us (3%)
    pallas_call x2, Pallas kernels, attend(): pl.pallas_call(functools.partial(attend_kernel, late), out_shape=out if l...  29.4 us
    all_to_all x1, waiting for transfers between devices, local(): lax.all_to_all(outgoing, SEQ_AXES, split_axis=0, concat_axis=0, tiled=True)  22.7 us
    all_to_all x1, blocking collectives, local(): lax.all_to_all(copies, HEAD_AXES, split_axis=0, concat_axis=0, tiled=True)  13.5 us
    ppermute x1, waiting for transfers between devices, local(): far_a = lax.ppermute(w_lo[:half], 'y', UP)  10.7 us
    all_to_all x1, waiting for transfers between devices, local(): lax.all_to_all(context, SEQ_AXES, split_axis=0, concat_axis=0, tiled=True)  10.1 us
    ppermute x1, waiting for transfers between devices, local(): x_lo_b = lax.ppermute(w_lo[half:], 'xl', SWAP)  7.76 us
    unnamed x22, local copies, waits for them, and re-layouts  5.89 us
    all_to_all x1, starting transfers between devices, local(): lax.all_to_all(outgoing, SEQ_AXES, split_axis=0, concat_axis=0, tiled=True)  4.61 us
  transfers between devices with their start and end apart: 23, of which 9 were waited for; matrix products, arithmetic and copies ran while one was open for 5% of the time, Pallas kernels for 20%

commit v1 on v0

--- a/solution.py
+++ b/solution.py
@@ -48,7 +48,7 @@
 
 
 LIMIT = pltpu.CompilerParams(vmem_limit_bytes=24 << 20)
-SMALL = pltpu.CompilerParams(vmem_limit_bytes=8 << 20)
+SMALL = pltpu.CompilerParams(vmem_limit_bytes=12 << 20)
 
 
 def dispatch_kernel(owner_ref, q_ref, out_ref, used):
@@ -111,14 +111,28 @@
     )(owners, *near(returned))
 
 
-def attend_kernel(late, order, first, meta, q_ref, *refs):
+def widen_kernel(kv_ref, out_ref):
+    out_ref[:, :HEAD_DIM] = kv_ref[0, 0]
+    out_ref[:, HEAD_DIM : 2 * HEAD_DIM] = kv_ref[0, 1]
+    out_ref[:, 2 * HEAD_DIM :] = jnp.ones((KEY_CAP, HEAD_DIM), jnp.bfloat16)
+
+
+def widen(image_kv):
+    return pl.pallas_call(
+        widen_kernel,
+        out_shape=pltpu.VMEM((KEY_CAP, 3 * HEAD_DIM), jnp.bfloat16),
+        in_specs=[vmem()],
+        out_specs=vmem(),
+        compiler_params=SMALL,
+        name="widen",
+    )(image_kv)
+
+
+def attend_kernel(late, order, first, meta, q_ref, kv_s, *refs):
     if late:
-        kv_s, _, o_ref, q_s, m_s, acc = refs
+        _, o_ref, q_s, m_s, acc = refs
     else:
-        kv_ref, o_ref, kv_s, q_keep, q_s, m_s, acc = refs
-        kv_s[:, :HEAD_DIM] = kv_ref[0, 0]
-        kv_s[:, HEAD_DIM : 2 * HEAD_DIM] = kv_ref[0, 1]
-        kv_s[:, 2 * HEAD_DIM :] = jnp.ones((KEY_CAP, HEAD_DIM), jnp.bfloat16)
+        o_ref, q_keep, q_s, m_s, acc = refs
         q_keep[...] = q_ref[...]
     groups = lax.shift_right_logical(meta[0] + GROUP - 1, 3)
     middle = lax.shift_right_logical(groups + 1, 1)
@@ -139,14 +153,22 @@
         def tile(t, inner):
             base = pl.multiple_of(t * TILE_STEP, BLK)
             keys = kv_s[pl.ds(base, KEY_BLK), :HEAD_DIM]
-            for u in range(rows // SUB):
-                part = slice(u * SUB, (u + 1) * SUB)
-                s = lax.dot_general(
-                    q_s[part, :],
+            blocks = rows // SUB
+
+            def scores(u):
+                return lax.dot_general(
+                    q_s[u * SUB : (u + 1) * SUB, :],
                     keys,
                     (((1,), (1,)), ((), ())),
                     preferred_element_type=jnp.float32,
                 )
+
+            ahead = scores(0)
+            for u in range(blocks):
+                part = slice(u * SUB, (u + 1) * SUB)
+                s = ahead
+                if u + 1 < blocks:
+                    ahead = scores(u + 1)
                 tail = KEY_BLK - HEAD_DIM
                 head_cols = jnp.where(col >= t, s[:, :HEAD_DIM], LOW)
                 tail_cols = jnp.where(col + tail < t + TILE_TOK, s[:, tail:], LOW)
@@ -191,23 +213,18 @@
         lax.fori_loop(0, middle, group, 0)
 
 
-def attend(order, first, meta, received=None, image_kv=None, earlier=None):
+def attend(order, first, meta, received, keys, context=None):
     rows = GROUP * HEADS_DEV * BLK
-    late = earlier is not None
+    late = context is not None
     out = pltpu.VMEM((SEQ // 2, 2, 2 * CAP, BLK, HEADS_DEV * HEAD_DIM // 2), jnp.bfloat16)
-    if late:
-        context, keys, slots = near(*earlier)
-        operands = (slots, keys, context)
-    else:
-        operands = (*near(received), image_kv)
-        keys = pltpu.VMEM((KEY_CAP, 3 * HEAD_DIM), jnp.bfloat16)
-        slots = pltpu.VMEM(received.shape, received.dtype)
+    slots = pltpu.VMEM(received.shape, received.dtype)
+    operands = near(received, keys, *([context] if late else []))
     return pl.pallas_call(
         functools.partial(attend_kernel, late),
-        out_shape=out if late else (out, keys, slots),
+        out_shape=out if late else (out, slots),
         input_output_aliases={5: 0} if late else {},
         in_specs=[smem()] * 3 + [vmem()] * len(operands),
-        out_specs=vmem() if late else (vmem(),) * 3,
+        out_specs=vmem() if late else (vmem(),) * 2,
         scratch_shapes=[
             pltpu.VMEM((rows, HEAD_DIM), jnp.bfloat16),
             pltpu.VMEM((rows, HEAD_DIM), jnp.float32),
@@ -278,14 +295,14 @@
     for block, dz, flip in ((below[...], 3, 1), (above[...], 1, 1), (far, 2, 0), (over, 2, 1)):
         full += jnp.dot(block, w[weight_spot(dz, flip)], preferred_element_type=jnp.float32)
     keep_ref[...] = full[:half]
-    give_ref[...] = full[half:]
+    give_ref[...] = full[half:].astype(jnp.bfloat16)
 
 
 def project_last(blocks, weights, total):
     shape = pltpu.VMEM((total.shape[0] // 2, total.shape[1]), jnp.float32)
     return pl.pallas_call(
         project_last_kernel,
-        out_shape=(shape, shape),
+        out_shape=(shape, pltpu.VMEM(shape.shape, jnp.bfloat16)),
         in_specs=[vmem()] * 8,
         out_specs=(vmem(), vmem()),
         compiler_params=LIMIT,
@@ -341,26 +358,21 @@
     tiles = lax.dynamic_index_in_dim(tile_counts, here, 0, keepdims=False)
     meta = jnp.stack([n_active, tiles])
     slots = received.reshape(SLOTS, BLK, width)
-    early = attend(order, first, meta, slots, image_kv)
-
-    far_a = lax.ppermute(w_lo[:half], "y", UP)
-    far_b = lax.ppermute(w_hi[half:], "y", DOWN)
-    x_lo_a = lax.ppermute(w_x[:half], "y", UP)
-    x_hi_a = lax.ppermute(w_x[:half], "y", DOWN)
-    x_lo_b = lax.ppermute(w_lo[half:], "xl", SWAP)
-    x_hi_b = lax.ppermute(w_hi[half:], "xl", SWAP)
-
-    context = attend(order, first, meta, earlier=early)
-
-    x_far_a = lax.ppermute(x_lo_a, "y", UP)
-    x_far_b = lax.ppermute(far_b, "xl", SWAP)
+    keys = widen(image_kv)
+    context, slots = attend(order, first, meta, slots, keys)
+
+    w_far = lax.ppermute(w_lo, "y", UP)
+    x_hi = lax.ppermute(w_x, "y", DOWN)
+    x_lo = lax.ppermute(w_lo, "xl", SWAP)
+
+    context = attend(order, first, meta, slots, keys, context)
+
+    x_far_a = lax.ppermute(w_far[:half], "xl", SWAP)
+    x_far_b = lax.ppermute(x_lo[half:], "y", UP)
 
     context = context.reshape(SEQ, 2 * CAP, BLK, width // 2)
     returned = lax.all_to_all(context, SEQ_AXES, split_axis=0, concat_axis=0, tiled=True)
-    weights = assemble(
-        (w, w_lo, w_hi, far_a, far_b)
-        + (w_x, x_lo_a, x_lo_b, x_hi_a, x_hi_b, x_far_a, x_far_b)
-    )
+    weights = assemble((w, w_lo, w_hi, w_far, w_x, x_lo, x_hi, x_far_a, x_far_b))
     own = collect(owners, returned)
     below = lax.ppermute(own, "z", UP)
     above = lax.ppermute(own, "z", DOWN)
@@ -375,7 +387,7 @@
     total = project_first(own, below, above, across, weights)
     blocks = (across_below, across_above, far_a, far_b, over_a, over_b)
     keep, give = project_last(blocks, weights, total)
-    branch = keep + lax.ppermute(give, "core", SWAP)
+    branch = keep + lax.ppermute(give, "core", SWAP).astype(jnp.float32)
 
     hidden_out = (hidden_in.astype(jnp.float32) + jnp.tanh(gate[0]) * branch).astype(jnp.bfloat16)
     hidden = hidden_out.astype(jnp.float32)

time: 180 us -> 177 us (0.983)
  local copies, waits for them, and re-layouts: 11.4 us -> 8.34 us
  Pallas kernels: 39 us -> 41.8 us
  starting transfers between devices: 43.8 us -> 41.3 us
    ppermute x1, waiting for transfers between devices: 0.01 us -> 9.15 us  [local(): below = lax.ppermute(own, 'z', UP)]
    ppermute x9 -> x6, waiting for transfers between devices: 27.5 us -> 20.2 us  [the longest x1 14.7 us: local(): x_lo = lax.ppermute(w_lo, 'xl', SWAP)]
    ppermute x1, waiting for transfers between devices: 0.01 us -> 4.03 us  [local(): far_a = lax.ppermute(below[:rows], 'z', UP)]
    ppermute x9 -> x6, starting transfers between devices: 10.9 us -> 7.09 us  [the longest x1 1.93 us: local(): x_lo = lax.ppermute(w_lo, 'xl', SWAP)]
    all_to_all x1, waiting for transfers between devices: 22.7 us -> 19.5 us  [local(): lax.all_to_all(outgoing, SEQ_AXES, split_axis=0, concat_axis=0, tiled=True)]
    slice x3 -> x2, local copies, waits for them, and re-layouts: 2.98 us -> 0.07 us  [the longest x1 0.03 us: local(): x_far_b = lax.ppermute(x_lo[half:], 'y', UP)]
    ppermute x1, waiting for transfers between devices: 2.81 us -> 0.01 us  [local(): over_a = lax.ppermute(far_a, 'xh', SWAP)]
    ppermute x1, starting transfers between devices: 4.04 us -> 1.81 us  [local(): far_b = lax.ppermute(above[rows:], 'z', DOWN)]
  transfers between devices with their start and end apart: 23 -> 20, of which waited for: 9 -> 8; matrix products, arithmetic and copies ran while one was open for 5% -> 3% of each run, Pallas kernels for 20% -> 22%
where the time goes in v1:
time: 177 us
  waiting for transfers between devices  65.1 us (37%)
  Pallas kernels  41.8 us (24%)
  starting transfers between devices  41.3 us (23%)
  blocking collectives  13 us (7%)
  local copies, waits for them, and re-layouts  8.34 us (5%)
  other arithmetic  5.4 us (3%)
    pallas_call x2, Pallas kernels, attend(): pl.pallas_call(functools.partial(attend_kernel, late), out_shape=out if l...  30.9 us
    all_to_all x1, waiting for transfers between devices, local(): lax.all_to_all(outgoing, SEQ_AXES, split_axis=0, concat_axis=0, tiled=True)  19.5 us
    ppermute x1, waiting for transfers between devices, local(): x_lo = lax.ppermute(w_lo, 'xl', SWAP)  14.7 us
    all_to_all x1, blocking collectives, local(): lax.all_to_all(copies, HEAD_AXES, split_axis=0, concat_axis=0, tiled=True)  13 us
    all_to_all x1, waiting for transfers between devices, local(): lax.all_to_all(context, SEQ_AXES, split_axis=0, concat_axis=0, tiled=True)  10.4 us
    ppermute x1, waiting for transfers between devices, local(): below = lax.ppermute(own, 'z', UP)  9.15 us
    unnamed x26, local copies, waits for them, and re-layouts  6.42 us
    all_to_all x1, starting transfers between devices, local(): lax.all_to_all(outgoing, SEQ_AXES, split_axis=0, concat_axis=0, tiled=True)  4.49 us
  transfers between devices with their start and end apart: 20, of which 8 were waited for; matrix products, arithmetic and copies ran while one was open for 3% of the time, Pallas kernels for 22%

profile of v1, /device:TPU:0, one launch (start us, length us, event | category | flops | bytes accessed | tf_op | source)
XLA Modules:
  0.0 176.6 jit_solution(4998164407733209617)
XLA Ops:
  0.6 1.8 collective-permute-start.9
  2.4 1.5 collective-permute-start.12
  3.9 1.0 copy-done.4
  4.9 0.7 copy-done.5
  5.6 1.7 dispatch.1
  7.3 4.5 %all-to-all-start = ((bf16[16,2,16,1024]{3,2,1,0:T(8,128)(2,1)}), bf16[16,2,16,1024]{3,2,1,0:T(8,128)(2,1)}, u32[]{:S(2)}, u32[]{:S(2)}) async-start(bf16[16,2,16,1024]{3,2,1,0:T(8,128)(2,1)} %dispatch.1), calls=%async_computation | async-start | bytes 2097152 | tf_op jit(solution)/shard_map/all_to_all | solution.py:351
  11.9 0.7 broadcast_compare_fusion
  12.6 0.4 convert_reduce_fusion
  13.3 0.8 broadcast_in_dim.57
  14.4 0.8 widen.1.kv_s
  15.2 2.2 %copy-done = bf16[6528,384]{1,0:T(8,128)(2,1)} copy-done((bf16[6528,384]{1,0:T(8,128)(2,1)}, bf16[6528,384]{1,0:T(8,128)(2,1)S(1)}, u32[]{:S(2)}) %copy-start) | copy-done | bytes 5013528
  17.4 0.6 dynamic_slice.4
  18.0 0.7 convert_reduce_fusion.2
  18.7 1.4 pad_add_fusion.meta
  20.0 0.2 convert_reduce_fusion.1
  20.3 19.5 %all-to-all-done = bf16[16,2,16,1024]{3,2,1,0:T(8,128)(2,1)} async-done(((bf16[16,2,16,1024]{3,2,1,0:T(8,128)(2,1)}), bf16[16,2,16,1024]{3,2,1,0:T(8,128)(2,1)}, u32[]{:S(2)}, u32[]{:S(2)}) %all-to-all-start) | async-done | bytes 1048608 | tf_op jit(solution)/shard_map/all_to_all | solution.py:351
  39.8 2.4 %copy-done.1 = bf16[6528,384]{1,0:T(8,128)(2,1)S(1)} copy-done((bf16[6528,384]{1,0:T(8,128)(2,1)S(1)}, bf16[6528,384]{1,0:T(8,128)(2,1)}, u32[]{:S(2)}) %copy-start.1) | copy-done | bytes 5013528
  42.2 19.0 %attend_early.1 = (bf16[8,2,4,16,512]{4,3,2,1,0:T(8,128)(2,1)}, bf16[32,16,1024]{2,1,0:T(8,128)(2,1)S(1)}) custom-call(s32[32]{0:T(128)S(1)} %get-tuple-element.13.order, s32[32]{0:T(128)S(1)} %get-tuple-element.12.first, s32[2]{0:T(128)S(1)} %pad_add_fusion.meta, bf16[32,16,1024]{2,1,0:T(8,128)(2,1)} %bitcast.2.q_ref, bf16[6528,384]{1,0:T(8,128)(2,1)S(1)} %copy-done.1), custom_call_target="tpu_custom_call" | custom-call | flops 10000000000 | bytes 10000000 | tf_op jit(solution)/shard_map/attend_early/pallas_call | solution.py:222
  61.2 11.9 %attend_late.1 = bf16[8,2,4,16,512]{4,3,2,1,0:T(8,128)(2,1)} custom-call(s32[32]{0:T(128)S(1)} %get-tuple-element.13.order, s32[32]{0:T(128)S(1)} %get-tuple-element.12.first, s32[2]{0:T(128)S(1)} %pad_add_fusion.meta, bf16[32,16,1024]{2,1,0:T(8,128)(2,1)S(1)} %get-tuple-element.6.q_ref, ...), custom_call_target="tpu_custom_call", output_to_operand_aliasing={{}: (5, {})} | custom-call | flops 10000000000 | bytes 10000000 | tf_op jit(solution)/shard_map/attend_late/pallas_call | solution.py:222
  73.1 3.7 %all-to-all-start.1 = ((bf16[16,4,16,512]{3,2,1,0:T(8,128)(2,1)}), bf16[16,4,16,512]{3,2,1,0:T(8,128)(2,1)S(1)}, u32[]{:S(2)}, u32[]{:S(2)}) async-start(bf16[16,4,16,512]{3,2,1,0:T(8,128)(2,1)} %bitcast.3), calls=%async_computation.1 | async-start | bytes 2097152 | tf_op jit(solution)/shard_map/all_to_all | solution.py:374
  76.8 1.9 %collective-permute-start.13 = (bf16[512,1024]{1,0:T(8,128)(2,1)}, bf16[512,1024]{1,0:T(8,128)(2,1)S(1)}, u32[]{:S(2)}, u32[]{:S(2)}) collective-permute-start(bf16[512,1024]{1,0:T(8,128)(2,1)} %collective-permute-done.9.refs_1_), channel_id=1, source_target_pairs={{0,64},{64,0},{1,65},{65,1},{2,66},{66,2},{3,67},{67,3},{4,68},{68... | collective-permute-start | bytes 3145736 | tf_op jit(solution)/shard_map/ppermute | solution.py:366
  78.7 1.5 collective-permute-start.11
  80.2 1.8 collective-permute-start.10
  82.0 1.5 collective-permute-start.14
  83.5 10.4 %all-to-all-done.1.c_ref = bf16[16,4,16,512]{3,2,1,0:T(8,128)(2,1)S(1)} async-done(((bf16[16,4,16,512]{3,2,1,0:T(8,128)(2,1)}), bf16[16,4,16,512]{3,2,1,0:T(8,128)(2,1)S(1)}, u32[]{:S(2)}, u32[]{:S(2)}) %all-to-all-start.1) | async-done | bytes 1048608 | tf_op jit(solution)/shard_map/all_to_all | solution.py:374
  93.9 1.0 collect.1.own
  94.9 4.1 %collective-permute-start.5 = (bf16[512,512]{1,0:T(8,128)(2,1)S(1)}, bf16[512,512]{1,0:T(8,128)(2,1)S(1)}, u32[]{:S(2)}, u32[]{:S(2)}) collective-permute-start(bf16[512,512]{1,0:T(8,128)(2,1)S(1)} %collect.1.own), channel_id=1, source_target_pairs={{0,6},{2,0},{4,2},{6,4},{1,7},{3,1},{5,3},{7,5},{8,14},{10,8},{12,... | collective-permute-start | bytes 1572872 | tf_op jit(solution)/shard_map/ppermute | solution.py:378
  99.0 14.7 %collective-permute-done.13.refs_5_ = bf16[512,1024]{1,0:T(8,128)(2,1)S(1)} collective-permute-done((bf16[512,1024]{1,0:T(8,128)(2,1)}, bf16[512,1024]{1,0:T(8,128)(2,1)S(1)}, u32[]{:S(2)}, u32[]{:S(2)}) %collective-permute-start.13) | collective-permute-done | bytes 1048608 | tf_op jit(solution)/shard_map/ppermute | solution.py:366
  113.6 1.9 %collective-permute-start.3 = (bf16[512,512]{1,0:T(8,128)(2,1)S(1)}, bf16[512,512]{1,0:T(8,128)(2,1)S(1)}, u32[]{:S(2)}, u32[]{:S(2)}) collective-permute-start(bf16[512,512]{1,0:T(8,128)(2,1)S(1)} %collect.1.own), channel_id=1, source_target_pairs={{0,2},{2,4},{4,6},{6,0},{1,3},{3,5},{5,7},{7,1},{8,10},{10,12},{12... | collective-permute-start | bytes 1572872 | tf_op jit(solution)/shard_map/ppermute | solution.py:377
  115.6 3.1 %collective-permute-start = (bf16[512,512]{1,0:T(8,128)(2,1)S(1)}, bf16[512,512]{1,0:T(8,128)(2,1)S(1)}, u32[]{:S(2)}, u32[]{:S(2)}) collective-permute-start(bf16[512,512]{1,0:T(8,128)(2,1)S(1)} %collect.1.own), channel_id=1, source_target_pairs={{0,1},{1,0},{2,3},{3,2},{4,5},{5,4},{6,7},{7,6},{8,9},{9,8},{10,11... | collective-permute-start | bytes 1572872 | tf_op jit(solution)/shard_map/ppermute | solution.py:379
  118.7 1.5 collective-permute-start.16
  120.2 9.2 %collective-permute-done.3.below = bf16[512,512]{1,0:T(8,128)(2,1)S(1)} collective-permute-done((bf16[512,512]{1,0:T(8,128)(2,1)S(1)}, bf16[512,512]{1,0:T(8,128)(2,1)S(1)}, u32[]{:S(2)}, u32[]{:S(2)}) %collective-permute-start.3) | collective-permute-done | bytes 524320 | tf_op jit(solution)/shard_map/ppermute | solution.py:377
  129.4 0.6 collective-permute-start.15
  130.0 1.8 %collective-permute-start.6 = (bf16[256,512]{1,0:T(8,128)(2,1)S(1)}, bf16[256,512]{1,0:T(8,128)(2,1)S(1)}, u32[]{:S(2)}, u32[]{:S(2)}) collective-permute-start(bf16[256,512]{1,0:T(8,128)(2,1)S(1)} %slice.17), channel_id=1, source_target_pairs={{0,6},{2,0},{4,2},{6,4},{1,7},{3,1},{5,3},{7,5},{8,14},{10,8},{12,... | collective-permute-start | bytes 786440 | tf_op jit(solution)/shard_map/ppermute | solution.py:382
  131.8 4.3 %collective-permute-done.14.refs_6_ = bf16[512,1024]{1,0:T(8,128)(2,1)} collective-permute-done((bf16[512,1024]{1,0:T(8,128)(2,1)}, bf16[512,1024]{1,0:T(8,128)(2,1)}, u32[]{:S(2)}, u32[]{:S(2)}) %collective-permute-start.14) | collective-permute-done | bytes 1048608 | tf_op jit(solution)/shard_map/ppermute | solution.py:365
  136.1 1.9 %collective-permute-start.4 = (bf16[256,512]{1,0:T(8,128)(2,1)S(1)}, bf16[256,512]{1,0:T(8,128)(2,1)S(1)}, u32[]{:S(2)}, u32[]{:S(2)}) collective-permute-start(bf16[256,512]{1,0:T(8,128)(2,1)S(1)} %slice.16), channel_id=1, source_target_pairs={{0,2},{2,4},{4,6},{6,0},{1,3},{3,5},{5,7},{7,1},{8,10},{10,12},{12... | collective-permute-start | bytes 786440 | tf_op jit(solution)/shard_map/ppermute | solution.py:381
  138.0 2.1 %collective-permute-start.2 = (bf16[512,512]{1,0:T(8,128)(2,1)S(1)}, bf16[512,512]{1,0:T(8,128)(2,1)S(1)}, u32[]{:S(2)}, u32[]{:S(2)}) collective-permute-start(bf16[512,512]{1,0:T(8,128)(2,1)S(1)} %collective-permute-done.across), channel_id=1, source_target_pairs={{0,6},{2,0},{4,2},{6,4},{1,7},{3,1},{5,3},{7,5},{8,14},{10,8},{12,... | collective-permute-start | bytes 1572872 | tf_op jit(solution)/shard_map/ppermute | solution.py:384
  140.2 3.1 %collective-permute-start.8 = (bf16[256,512]{1,0:T(8,128)(2,1)S(1)}, bf16[256,512]{1,0:T(8,128)(2,1)S(1)}, u32[]{:S(2)}, u32[]{:S(2)}) collective-permute-start(bf16[256,512]{1,0:T(8,128)(2,1)S(1)} %collective-permute-done.6.far_b), channel_id=1, source_target_pairs={{0,1},{1,0},{2,3},{3,2},{4,5},{5,4},{6,7},{7,6},{8,9},{9,8},{10,11... | collective-permute-start | bytes 786440 | tf_op jit(solution)/shard_map/ppermute | solution.py:386
  143.3 4.0 %collective-permute-done.4.far_a = bf16[256,512]{1,0:T(8,128)(2,1)S(1)} collective-permute-done((bf16[256,512]{1,0:T(8,128)(2,1)S(1)}, bf16[256,512]{1,0:T(8,128)(2,1)S(1)}, u32[]{:S(2)}, u32[]{:S(2)}) %collective-permute-start.4) | collective-permute-done | bytes 262176 | tf_op jit(solution)/shard_map/ppermute | solution.py:381
  147.3 3.0 %collective-permute-start.7 = (bf16[256,512]{1,0:T(8,128)(2,1)S(1)}, bf16[256,512]{1,0:T(8,128)(2,1)S(1)}, u32[]{:S(2)}, u32[]{:S(2)}) collective-permute-start(bf16[256,512]{1,0:T(8,128)(2,1)S(1)} %collective-permute-done.4.far_a), channel_id=1, source_target_pairs={{0,1},{1,0},{2,3},{3,2},{4,5},{5,4},{6,7},{7,6},{8,9},{9,8},{10,11... | collective-permute-start | bytes 786440 | tf_op jit(solution)/shard_map/ppermute | solution.py:385
  150.3 2.7 %assemble.1.w = bf16[8,512,1024]{2,1,0:T(8,128)(2,1)S(1)} custom-call(bf16[512,1024]{1,0:T(8,128)(2,1)S(1)} %copy-done.3, bf16[512,1024]{1,0:T(8,128)(2,1)} %collective-permute-done.9.refs_1_, bf16[512,1024]{1,0:T(8,128)(2,1)} %collective-permute-done.10.refs_2_, bf16[512,1024]{1,0:T(8,128)(2,1)S(1)} %collective-permute-done.11.refs_3_, ...), custom_call_target="tpu_custom_call" | custom-call | tf_op jit(solution)/shard_map/assemble/pallas_call | solution.py:256
  153.1 2.3 %project_first.1.total = f32[512,1024]{1,0:T(8,128)S(1)} custom-call(bf16[512,512]{1,0:T(8,128)(2,1)S(1)} %collect.1.own, bf16[512,512]{1,0:T(8,128)(2,1)S(1)} %collective-permute-done.3.below, bf16[512,512]{1,0:T(8,128)(2,1)S(1)} %collective-permute-done.5.above, bf16[512,512]{1,0:T(8,128)(2,1)S(1)} %collective-permute-done.across, ...), custom_call_target="tpu_custom_call" | custom-call | tf_op jit(solution)/shard_map/project_first/pallas_call | solution.py:280
  155.5 1.9 %collective-permute-done.1.below = bf16[512,512]{1,0:T(8,128)(2,1)S(1)} collective-permute-done((bf16[512,512]{1,0:T(8,128)(2,1)S(1)}, bf16[512,512]{1,0:T(8,128)(2,1)S(1)}, u32[]{:S(2)}, u32[]{:S(2)}) %collective-permute-start.1) | collective-permute-done | bytes 524320 | tf_op jit(solution)/shard_map/ppermute | solution.py:383
  157.4 2.3 %project_last.1 = (f32[256,1024]{1,0:T(8,128)S(1)}, bf16[256,1024]{1,0:T(8,128)(2,1)S(1)}) custom-call(bf16[512,512]{1,0:T(8,128)(2,1)S(1)} %collective-permute-done.1.below, bf16[512,512]{1,0:T(8,128)(2,1)S(1)} %collective-permute-done.2.above, bf16[256,512]{1,0:T(8,128)(2,1)S(1)} %collective-permute-done.4.far_a, ...), custom_call_target="tpu_custom_call" | custom-call | tf_op jit(solution)/shard_map/project_last/pallas_call | solution.py:303
  160.5 1.2 collective-permute-done.17
  161.7 0.5 fusion
  162.3 13.0 %all_to_all.15 = f32[8,2,256]{2,1,0:T(2,128)S(1)} all-to-all(f32[8,2,256]{2,1,0:T(2,128)S(1)} %broadcast_in_dim.64), channel_id=1, replica_groups=mesh['xl'=2,'y'=4,'core'=2,'z'=4,'xh'=2] {'z','xh'}, dimensions={0} | all-to-all | bytes 32768 | tf_op jit(solution)/shard_map/all_to_all | solution.py:397
  175.3 1.3 fusion.2
  (55 shorter events, 1.2 us)
Async XLA Ops:
  0.6 13.8 %copy-start.2 = (bf16[1,2,6528,128]{3,2,1,0:T(8,128)(2,1)S(1)}, bf16[1,2,6528,128]{3,2,1,0:T(8,128)(2,1)}, u32[]{:S(2)}) copy-start(bf16[1,2,6528,128]{3,2,1,0:T(8,128)(2,1)} %kv_ref.1) | copy-start | bytes 10027012
  0.6 76.2 %collective-permute-start.9 = (bf16[512,1024]{1,0:T(8,128)(2,1)}, bf16[512,1024]{1,0:T(8,128)(2,1)}, u32[]{:S(2)}, u32[]{:S(2)}) collective-permute-start(bf16[512,1024]{1,0:T(8,128)(2,1)} %refs_0_.1), channel_id=1, source_target_pairs={{0,16},{16,32},{32,48},{48,0},{1,17},{17,33},{33,49},{49,1},{2,18}... | collective-permute-start | bytes 3145736 | tf_op jit(solution)/shard_map/ppermute | solution.py:353
  2.4 79.6 %collective-permute-start.12 = (bf16[512,1024]{1,0:T(8,128)(2,1)}, bf16[512,1024]{1,0:T(8,128)(2,1)}, u32[]{:S(2)}, u32[]{:S(2)}) collective-permute-start(bf16[512,1024]{1,0:T(8,128)(2,1)} %refs_0_.1), channel_id=1, source_target_pairs={{0,64},{64,0},{1,65},{65,1},{2,66},{66,2},{3,67},{67,3},{4,68},{68... | collective-permute-start | bytes 3145736 | tf_op jit(solution)/shard_map/ppermute | solution.py:355
  3.9 1.0 copy-start.4
  4.9 0.7 copy-start.5
  7.3 10.1 %copy-start.12 = (s32[16]{0:T(128)S(1)}, s32[16]{0:T(128)}, u32[]{:S(2)}) copy-start(s32[16]{0:T(128)} %param.16) | copy-start | bytes 196
  7.3 32.5 %all-to-all-start = ((bf16[16,2,16,1024]{3,2,1,0:T(8,128)(2,1)}), bf16[16,2,16,1024]{3,2,1,0:T(8,128)(2,1)}, u32[]{:S(2)}, u32[]{:S(2)}) async-start(bf16[16,2,16,1024]{3,2,1,0:T(8,128)(2,1)} %dispatch.1), calls=%async_computation | async-start | bytes 2097152 | tf_op jit(solution)/shard_map/all_to_all | solution.py:351
  15.2 2.2 %copy-start = (bf16[6528,384]{1,0:T(8,128)(2,1)}, bf16[6528,384]{1,0:T(8,128)(2,1)S(1)}, u32[]{:S(2)}) copy-start(bf16[6528,384]{1,0:T(8,128)(2,1)S(1)} %widen.1.kv_s) | copy-start | bytes 15040516
  39.8 2.4 %copy-start.1 = (bf16[6528,384]{1,0:T(8,128)(2,1)S(1)}, bf16[6528,384]{1,0:T(8,128)(2,1)}, u32[]{:S(2)}) copy-start(bf16[6528,384]{1,0:T(8,128)(2,1)} %copy-done) | copy-start | bytes 15040516
  61.2 32.7 %copy-start.6 = (s32[256]{0:T(256)S(1)}, s32[256]{0:T(256)}, u32[]{:S(2)}) copy-start(s32[256]{0:T(256)} %owner_ref.3) | copy-start | bytes 3076
  73.1 20.7 %all-to-all-start.1 = ((bf16[16,4,16,512]{3,2,1,0:T(8,128)(2,1)}), bf16[16,4,16,512]{3,2,1,0:T(8,128)(2,1)S(1)}, u32[]{:S(2)}, u32[]{:S(2)}) async-start(bf16[16,4,16,512]{3,2,1,0:T(8,128)(2,1)} %bitcast.3), calls=%async_computation.1 | async-start | bytes 2097152 | tf_op jit(solution)/shard_map/all_to_all | solution.py:374
  76.8 36.8 %collective-permute-start.13 = (bf16[512,1024]{1,0:T(8,128)(2,1)}, bf16[512,1024]{1,0:T(8,128)(2,1)S(1)}, u32[]{:S(2)}, u32[]{:S(2)}) collective-permute-start(bf16[512,1024]{1,0:T(8,128)(2,1)} %collective-permute-done.9.refs_1_), channel_id=1, source_target_pairs={{0,64},{64,0},{1,65},{65,1},{2,66},{66,2},{3,67},{67,3},{4,68},{68... | collective-permute-start | bytes 3145736 | tf_op jit(solution)/shard_map/ppermute | solution.py:366
  78.7 36.8 %collective-permute-start.11 = (bf16[512,1024]{1,0:T(8,128)(2,1)}, bf16[512,1024]{1,0:T(8,128)(2,1)S(1)}, u32[]{:S(2)}, u32[]{:S(2)}) collective-permute-start(bf16[512,1024]{1,0:T(8,128)(2,1)} %collective-permute-done.9.refs_1_), channel_id=1, source_target_pairs={{0,16},{16,32},{32,48},{48,0},{1,17},{17,33},{33,49},{49,1},{2,18}... | collective-permute-start | bytes 3145736 | tf_op jit(solution)/shard_map/ppermute | solution.py:364
  80.2 49.8 %collective-permute-start.10 = (bf16[512,1024]{1,0:T(8,128)(2,1)}, bf16[512,1024]{1,0:T(8,128)(2,1)}, u32[]{:S(2)}, u32[]{:S(2)}) collective-permute-start(bf16[512,1024]{1,0:T(8,128)(2,1)} %refs_0_.1), channel_id=1, source_target_pairs={{0,48},{16,0},{32,16},{48,32},{1,49},{17,1},{33,17},{49,33},{2,50}... | collective-permute-start | bytes 3145736 | tf_op jit(solution)/shard_map/ppermute | solution.py:354
  82.0 54.1 %collective-permute-start.14 = (bf16[512,1024]{1,0:T(8,128)(2,1)}, bf16[512,1024]{1,0:T(8,128)(2,1)}, u32[]{:S(2)}, u32[]{:S(2)}) collective-permute-start(bf16[512,1024]{1,0:T(8,128)(2,1)} %collective-permute-done.12.refs_4_), channel_id=1, source_target_pairs={{0,48},{16,0},{32,16},{48,32},{1,49},{17,1},{33,17},{49,33},{2,50}... | collective-permute-start | bytes 3145736 | tf_op jit(solution)/shard_map/ppermute | solution.py:365
  93.9 56.5 %copy-start.3 = (bf16[512,1024]{1,0:T(8,128)(2,1)S(1)}, bf16[512,1024]{1,0:T(8,128)(2,1)}, u32[]{:S(2)}) copy-start(bf16[512,1024]{1,0:T(8,128)(2,1)} %refs_0_.1) | copy-start | bytes 3145732
  94.9 23.8 %collective-permute-start.5 = (bf16[512,512]{1,0:T(8,128)(2,1)S(1)}, bf16[512,512]{1,0:T(8,128)(2,1)S(1)}, u32[]{:S(2)}, u32[]{:S(2)}) collective-permute-start(bf16[512,512]{1,0:T(8,128)(2,1)S(1)} %collect.1.own), channel_id=1, source_target_pairs={{0,6},{2,0},{4,2},{6,4},{1,7},{3,1},{5,3},{7,5},{8,14},{10,8},{12,... | collective-permute-start | bytes 1572872 | tf_op jit(solution)/shard_map/ppermute | solution.py:378
  113.6 15.8 %collective-permute-start.3 = (bf16[512,512]{1,0:T(8,128)(2,1)S(1)}, bf16[512,512]{1,0:T(8,128)(2,1)S(1)}, u32[]{:S(2)}, u32[]{:S(2)}) collective-permute-start(bf16[512,512]{1,0:T(8,128)(2,1)S(1)} %collect.1.own), channel_id=1, source_target_pairs={{0,2},{2,4},{4,6},{6,0},{1,3},{3,5},{5,7},{7,1},{8,10},{10,12},{12... | collective-permute-start | bytes 1572872 | tf_op jit(solution)/shard_map/ppermute | solution.py:377
  115.6 22.5 %collective-permute-start = (bf16[512,512]{1,0:T(8,128)(2,1)S(1)}, bf16[512,512]{1,0:T(8,128)(2,1)S(1)}, u32[]{:S(2)}, u32[]{:S(2)}) collective-permute-start(bf16[512,512]{1,0:T(8,128)(2,1)S(1)} %collect.1.own), channel_id=1, source_target_pairs={{0,1},{1,0},{2,3},{3,2},{4,5},{5,4},{6,7},{7,6},{8,9},{9,8},{10,11... | collective-permute-start | bytes 1572872 | tf_op jit(solution)/shard_map/ppermute | solution.py:379
  118.7 21.5 %collective-permute-start.16 = (bf16[256,1024]{1,0:T(8,128)(2,1)S(1)}, bf16[256,1024]{1,0:T(8,128)(2,1)S(1)}, u32[]{:S(2)}, u32[]{:S(2)}) collective-permute-start(bf16[256,1024]{1,0:T(8,128)(2,1)S(1)} %slice.19), channel_id=1, source_target_pairs={{0,16},{16,32},{32,48},{48,0},{1,17},{17,33},{33,49},{49,1},{2,18}... | collective-permute-start | bytes 1572872 | tf_op jit(solution)/shard_map/ppermute | solution.py:371
  129.4 20.9 %collective-permute-start.15 = (bf16[256,1024]{1,0:T(8,128)(2,1)S(1)}, bf16[256,1024]{1,0:T(8,128)(2,1)S(1)}, u32[]{:S(2)}, u32[]{:S(2)}) collective-permute-start(bf16[256,1024]{1,0:T(8,128)(2,1)S(1)} %slice.18), channel_id=1, source_target_pairs={{0,64},{64,0},{1,65},{65,1},{2,66},{66,2},{3,67},{67,3},{4,68},{68... | collective-permute-start | bytes 1572872 | tf_op jit(solution)/shard_map/ppermute | solution.py:370
  130.0 10.1 %collective-permute-start.6 = (bf16[256,512]{1,0:T(8,128)(2,1)S(1)}, bf16[256,512]{1,0:T(8,128)(2,1)S(1)}, u32[]{:S(2)}, u32[]{:S(2)}) collective-permute-start(bf16[256,512]{1,0:T(8,128)(2,1)S(1)} %slice.17), channel_id=1, source_target_pairs={{0,6},{2,0},{4,2},{6,4},{1,7},{3,1},{5,3},{7,5},{8,14},{10,8},{12,... | collective-permute-start | bytes 786440 | tf_op jit(solution)/shard_map/ppermute | solution.py:382
  136.1 11.2 %collective-permute-start.4 = (bf16[256,512]{1,0:T(8,128)(2,1)S(1)}, bf16[256,512]{1,0:T(8,128)(2,1)S(1)}, u32[]{:S(2)}, u32[]{:S(2)}) collective-permute-start(bf16[256,512]{1,0:T(8,128)(2,1)S(1)} %slice.16), channel_id=1, source_target_pairs={{0,2},{2,4},{4,6},{6,0},{1,3},{3,5},{5,7},{7,1},{8,10},{10,12},{12... | collective-permute-start | bytes 786440 | tf_op jit(solution)/shard_map/ppermute | solution.py:381
  138.0 17.4 %collective-permute-start.2 = (bf16[512,512]{1,0:T(8,128)(2,1)S(1)}, bf16[512,512]{1,0:T(8,128)(2,1)S(1)}, u32[]{:S(2)}, u32[]{:S(2)}) collective-permute-start(bf16[512,512]{1,0:T(8,128)(2,1)S(1)} %collective-permute-done.across), channel_id=1, source_target_pairs={{0,6},{2,0},{4,2},{6,4},{1,7},{3,1},{5,3},{7,5},{8,14},{10,8},{12,... | collective-permute-start | bytes 1572872 | tf_op jit(solution)/shard_map/ppermute | solution.py:384
  140.2 17.2 %collective-permute-start.1 = (bf16[512,512]{1,0:T(8,128)(2,1)S(1)}, bf16[512,512]{1,0:T(8,128)(2,1)S(1)}, u32[]{:S(2)}, u32[]{:S(2)}) collective-permute-start(bf16[512,512]{1,0:T(8,128)(2,1)S(1)} %collective-permute-done.across), channel_id=1, source_target_pairs={{0,2},{2,4},{4,6},{6,0},{1,3},{3,5},{5,7},{7,1},{8,10},{10,12},{12... | collective-permute-start | bytes 1572872 | tf_op jit(solution)/shard_map/ppermute | solution.py:383
  140.2 15.3 %collective-permute-start.8 = (bf16[256,512]{1,0:T(8,128)(2,1)S(1)}, bf16[256,512]{1,0:T(8,128)(2,1)S(1)}, u32[]{:S(2)}, u32[]{:S(2)}) collective-permute-start(bf16[256,512]{1,0:T(8,128)(2,1)S(1)} %collective-permute-done.6.far_b), channel_id=1, source_target_pairs={{0,1},{1,0},{2,3},{3,2},{4,5},{5,4},{6,7},{7,6},{8,9},{9,8},{10,11... | collective-permute-start | bytes 786440 | tf_op jit(solution)/shard_map/ppermute | solution.py:386
  147.3 8.2 %collective-permute-start.7 = (bf16[256,512]{1,0:T(8,128)(2,1)S(1)}, bf16[256,512]{1,0:T(8,128)(2,1)S(1)}, u32[]{:S(2)}, u32[]{:S(2)}) collective-permute-start(bf16[256,512]{1,0:T(8,128)(2,1)S(1)} %collective-permute-done.4.far_a), channel_id=1, source_target_pairs={{0,1},{1,0},{2,3},{3,2},{4,5},{5,4},{6,7},{7,6},{8,9},{9,8},{10,11... | collective-permute-start | bytes 786440 | tf_op jit(solution)/shard_map/ppermute | solution.py:385
  155.4 6.3 %copy-start.7 = (bf16[256,1024]{1,0:T(8,128)(2,1)S(1)}, bf16[256,1024]{1,0:T(8,128)(2,1)}, u32[]{:S(2)}) copy-start(bf16[256,1024]{1,0:T(8,128)(2,1)} %param.20) | copy-start | bytes 1572868
  155.4 6.3 %copy-start.9 = (bf16[256,1024]{1,0:T(8,128)(2,1)S(1)}, bf16[256,1024]{1,0:T(8,128)(2,1)}, u32[]{:S(2)}) copy-start(bf16[256,1024]{1,0:T(8,128)(2,1)} %param.11) | copy-start | bytes 1572868
  155.4 6.3 %copy-start.11 = (f32[1024]{0:T(1024)S(1)}, f32[1024]{0:T(1024)}, u32[]{:S(2)}) copy-start(f32[1024]{0:T(1024)} %param.19) | copy-start | bytes 12292
  155.5 19.8 %copy-start.10 = (bf16[256,1024]{1,0:T(8,128)(2,1)S(1)}, bf16[256,1024]{1,0:T(8,128)(2,1)}, u32[]{:S(2)}) copy-start(bf16[256,1024]{1,0:T(8,128)(2,1)} %param.21) | copy-start | bytes 1572868
  159.7 2.0 %collective-permute-start.17 = (bf16[256,1024]{1,0:T(8,128)(2,1)S(1)}, bf16[256,1024]{1,0:T(8,128)(2,1)S(1)}, u32[]{:S(2)}, u32[]{:S(2)}) collective-permute-start(bf16[256,1024]{1,0:T(8,128)(2,1)S(1)} %get-tuple-element.9), channel_id=1, source_target_pairs={{0,8},{8,0},{1,9},{9,1},{2,10},{10,2},{3,11},{11,3},{4,12},{12,4},... | collective-permute-start | bytes 1572872 | tf_op jit(solution)/shard_map/ppermute | solution.py:390
  162.2 14.4 %copy-start.8 = (bf16[256,1024]{1,0:T(8,128)(2,1)}, bf16[256,1024]{1,0:T(8,128)(2,1)S(1)}, u32[]{:S(2)}) copy-start(bf16[256,1024]{1,0:T(8,128)(2,1)S(1)} %get-tuple-element.14) | copy-start | bytes 1572868
